TPU v7x, 128 devices: a whole 4x4x4 slice. The times are simulated.
128 devices in a mesh: pts: 16 (over z, y), freq: 8 (over x, core).
Axes of the slice: x: 4, y: 4, z: 4, core: 2. Of those that a mesh axis runs over, the one named last changes fastest.
Arguments:
- spectra: bfloat16 [128, 5, 4096, 128], P('freq', None, 'pts'), parts along dimension 0, may hold values from -200 to 200, as said below
- weights: float32 [4096], P('pts'), as said below
Outputs:
- mode_shapes: bfloat16 [128, 5, 4096, 128], P('freq', None, 'pts'), parts along dimension 0
There are 8 independent parts, one for each index of `freq`. A program takes and returns all parts, laid end to end along the dimension named above; an argument that names none is the same for every part. Nothing has to cross between parts.
Inputs may be any that keep to these rules, and one draw needn't show every extreme that they name: `spectra`: each row (frequency, variable, point) and each block's column pair has its own scale; the complex columns are independent. `weights`: Positive; their sum is of order one.
All inputs are finite; a program needn't handle non-finite values.
Results may differ from a plain program's by a relative error of at most 0.0054.
Values sent between devices are 32-bit elements; how exact they have to be, the bound alone decides.
No kernel may reach another device: no remote copies, remote signals or barrier semaphores. Data moves between devices by JAX's collectives and lax.ppermute only.
A program may use at most 64 MiB of HBM per device.

v0:
```python
import jax
import jax.numpy as jnp
from jax import lax
from jax.sharding import PartitionSpec as P

NS_STEPS = 10


def split_parts(products):
    half_cols = products.shape[-1] // 2
    top_left = products[:, :half_cols, :half_cols]
    top_right = products[:, :half_cols, half_cols:]
    bottom_left = products[:, half_cols:, :half_cols]
    bottom_right = products[:, half_cols:, half_cols:]
    return (top_left + bottom_right, top_right - bottom_left)


def build_cross(real_part, imag_part):
    upper_row = jnp.concatenate([real_part, imag_part], 2)
    lower_row = jnp.concatenate([-imag_part, real_part], 2)
    return jnp.concatenate([upper_row, lower_row], 1)


def upper_of(cross_gram):
    order = cross_gram.shape[-1]
    places = jnp.arange(order)

    def eliminate(column, carry):
        working, factor = carry
        picker = (places == column).astype(jnp.float32)
        below = (places >= column).astype(jnp.float32)
        current = jnp.sum(working * picker[None, None, :], axis=2) * below[None, :]
        pivot = jnp.sqrt(jnp.sum(current * picker[None, :], axis=1))
        scaled = current / pivot[:, None]
        factor = factor + scaled[:, None, :] * picker[None, :, None]
        working = working - scaled[:, :, None] * scaled[:, None, :]
        return (working, factor)

    start = (cross_gram, jnp.zeros_like(cross_gram))
    working, factor = lax.fori_loop(0, order, eliminate, start)
    return factor


def solve_upper(upper_factor, right_side):
    order = upper_factor.shape[-1]
    places = jnp.arange(order)

    def back_step(count, solved):
        row = order - 1 - count
        picker = (places == row).astype(jnp.float32)
        factor_row = jnp.sum(upper_factor * picker[None, :, None], axis=1)
        side_row = jnp.sum(right_side * picker[None, :, None], axis=1)
        pivot = jnp.sum(factor_row * picker[None, :], axis=1)
        known = jnp.einsum("fj,fjk->fk", factor_row, solved, precision=lax.Precision.HIGHEST)
        value = (side_row - known) / pivot[:, None]
        return solved + picker[None, :, None] * value[:, None, :]

    return lax.fori_loop(0, order, back_step, jnp.zeros_like(right_side))


def gram_of(upper_factor):
    return jnp.einsum("fki,fkj->fij", upper_factor, upper_factor, precision=lax.Precision.HIGHEST)


def local(spectra, weights):
    freq_count, var_count, point_count, col_count = spectra.shape
    root_weights = jnp.sqrt(weights)
    weighted = (root_weights[None, None, :, None] * spectra.astype(jnp.float32)).astype(
        jnp.bfloat16
    )
    flat_rows = weighted.reshape(freq_count, var_count * point_count, col_count)
    products = jnp.einsum("frc,frd->fcd", flat_rows, flat_rows, preferred_element_type=jnp.float32)
    real_part, imag_part = split_parts(products)
    cross_gram = build_cross(real_part, imag_part)
    summed = lax.psum(cross_gram, "pts")
    upper_factor = upper_of(summed)
    frob_norm = jnp.sqrt(jnp.sum(upper_factor * upper_factor, axis=(1, 2)))
    polar = upper_factor / frob_norm[:, None, None]
    for sweep in range(NS_STEPS):
        inner_gram = gram_of(polar)
        polar = 1.5 * polar - 0.5 * jnp.einsum(
            "fij,fjk->fik", polar, inner_gram, precision=lax.Precision.HIGHEST
        )
    mapping = solve_upper(upper_factor, polar).astype(jnp.bfloat16)
    shapes = jnp.einsum("fvpc,fcd->fvpd", spectra, mapping, preferred_element_type=jnp.float32)
    return shapes.astype(jnp.bfloat16)


def solution(mesh):
    in_specs = (P("freq", None, "pts", None), P("pts"))
    out_specs = P("freq", None, "pts", None)
    return jax.shard_map(local, mesh=mesh, in_specs=in_specs, out_specs=out_specs, check_vma=False)
```

profile of v0, /device:TPU:0, one launch (start us, length us, event | category | flops | bytes accessed | tf_op | source)
XLA Modules:
  0.0 935.5 jit_solution(8490604428545319796)
XLA Ops:
  7.2 4.0 multiply_convert_fusion
  14.6 90.1 %all-reduce.2.cloned.1.call-done = f32[16,128,128]{2,1,0:T(8,128)} async-done(((f32[16,128,128]{2,1,0:T(8,128)}), f32[16,128,128]{2,1,0:T(8,128)}) %all-reduce.2.cloned.1.call-update) | async-done | bytes 1048592 | tf_op jit(solution)/shard_map/psum | solution.py:75
  104.7 568.0 %while.32 = (s32[]{:T(128)}, f32[16,128,128]{2,1,0:T(8,128)}, f32[16,128,128]{2,1,0:T(8,128)S(1)}, s32[]{:T(128)}, s32[]{:T(128)}) while((s32[]{:T(128)}, f32[16,128,128]{2,1,0:T(8,128)}, f32[16,128,128]{2,1,0:T(8,128)S(1)}, s32[]{:T(128)}, s32[]{:T(128)}) %tuple.73), condition=%wide.region_4.0_spmd.clone.clone, body=%wide.region_1.0_spmd.clone.clone.sunk | while | flops 1843699 | bytes 5287763 | solution.py:40
  106.5 2.7 select_add_fusion.2
  110.9 2.7 select_add_fusion.2
  115.3 2.7 select_add_fusion.2
  124.2 2.7 select_add_fusion.2
  133.1 2.7 select_add_fusion.2
  137.5 2.7 select_add_fusion.2
  141.9 2.7 select_add_fusion.2
  146.4 2.7 select_add_fusion.2
  150.8 2.7 select_add_fusion.2
  155.2 2.7 select_add_fusion.2
  159.7 2.7 select_add_fusion.2
  164.1 2.7 select_add_fusion.2
  168.5 2.7 select_add_fusion.2
  173.0 2.7 select_add_fusion.2
  177.4 2.7 select_add_fusion.2
  181.8 2.7 select_add_fusion.2
  186.3 2.7 select_add_fusion.2
  190.7 2.7 select_add_fusion.2
  195.1 2.7 select_add_fusion.2
  199.6 2.7 select_add_fusion.2
  208.4 2.7 select_add_fusion.2
  217.3 2.7 select_add_fusion.2
  221.7 2.7 select_add_fusion.2
  226.2 2.7 select_add_fusion.2
  230.6 2.7 select_add_fusion.2
  235.0 2.7 select_add_fusion.2
  239.5 2.7 select_add_fusion.2
  243.9 2.7 select_add_fusion.2
  248.3 2.7 select_add_fusion.2
  252.8 2.7 select_add_fusion.2
  257.2 2.7 select_add_fusion.2
  261.7 2.7 select_add_fusion.2
  266.1 2.7 select_add_fusion.2
  270.5 2.7 select_add_fusion.2
  275.0 2.7 select_add_fusion.2
  279.4 2.7 select_add_fusion.2
  283.8 2.7 select_add_fusion.2
  292.7 2.7 select_add_fusion.2
  301.6 2.7 select_add_fusion.2
  306.0 2.7 select_add_fusion.2
  310.4 2.7 select_add_fusion.2
  314.9 2.7 select_add_fusion.2
  705.7 208.5 %while.31 = (s32[]{:T(128)}, f32[16,128,128]{2,1,0:T(8,128)S(1)}, f32[16,128,128]{2,1,0:T(8,128)S(1)}, f32[16,128,128]{2,1,0:T(8,128)S(1)}, s32[]{:T(128)}, /*index=5*/s32[]{:T(128)}, s32[]{:T(128)}) while((s32[]{:T(128)}, f32[16,128,128]{2,1,0:T(8,128)S(1)}, f32[16,128,128]{2,1,0:T(8,128)S(1)}, f32[16,128,128]{2,1,0:T(8,128)S(1)}, ...), condition=%wide.region_10.0_spmd.clone, body=%wide.region_6.0_spmd.clone.sunk | while | flops 5247220 | bytes 5318896 | solution.py:58
  914.2 6.4 convert_bitcast_fusion
  920.6 7.8 copy.8
  (1524 shorter events, 695.3 us)
Async XLA Ops:
  6.5 98.1 %all-reduce.2.cloned.1.call-start = ((), (), s32[]{:S(2)}) async-start(), calls=%async_computation | async-start | bytes 2097152 | tf_op jit(solution)/shard_map/psum | solution.py:75
Sparse Core Ops, SparseCore 0:
  14.7 89.9 all-reduce.1
where the time goes:
time: 950 us; the launch traced here: 936 us
  other arithmetic  655 us (69%)
  matrix products  160 us (17%)
  waiting for transfers between devices  90.1 us (9%)
  between operations  13.8 us (1%)
  local copies, waits for them, and re-layouts  9.6 us (1%)
    add x128, other arithmetic, eliminate(): factor = factor + scaled[:, None, :] * picker[None, :, None]  340 us
    reduce_sum x128, other arithmetic, eliminate(): current = jnp.sum(working * picker[None, None, :], axis=2) * below[None, :]  200 us
    dot_general x128, matrix products, back_step(): jnp.einsum('fj,fjk->fk', factor_row, solved, precision=lax.Precision.HIGH...  120 us
    psum x1, waiting for transfers between devices, local(): summed = lax.psum(cross_gram, 'pts')  90.1 us
    reduce_sum x128, other arithmetic, back_step(): factor_row = jnp.sum(upper_factor * picker[None, :, None], axis=1)  33.5 us
    add x128, other arithmetic, back_step(): return solved + picker[None, :, None] * value[:, None, :]  25.6 us
    dot_general x10, matrix products, gram_of(): jnp.einsum('fki,fkj->fij', upper_factor, upper_factor, precision=lax.Prec...  19.4 us
  transfers between devices with their start and end apart: 1, of which 1 were waited for; matrix products, arithmetic and copies ran while one was open for 0% of the time, Pallas kernels for 0%

commit v1 on v0

--- a/solution.py
+++ b/solution.py
@@ -72,7 +72,8 @@
     products = jnp.einsum("frc,frd->fcd", flat_rows, flat_rows, preferred_element_type=jnp.float32)
     real_part, imag_part = split_parts(products)
     cross_gram = build_cross(real_part, imag_part)
-    summed = lax.psum(cross_gram, "pts")
+    parts = lax.all_gather(cross_gram, "pts", axis=0, tiled=False)
+    summed = parts.sum(axis=0)
     upper_factor = upper_of(summed)
     frob_norm = jnp.sqrt(jnp.sum(upper_factor * upper_factor, axis=(1, 2)))
     polar = upper_factor / frob_norm[:, None, None]

time: 950 us -> 563 us (0.59)
  other arithmetic: 655 us -> 249 us
  waiting for transfers between devices: 90.1 us -> 114 us
    add x128, other arithmetic: 340 us -> 81.9 us  [eliminate(): factor = factor + scaled[:, None, :] * picker[None, :, None]]
    reduce_sum x128, other arithmetic: 200 us -> 44.1 us  [eliminate(): current = jnp.sum(working * picker[None, None, :], axis=2) * below[None, :]]
    all_gather x0 -> x1, waiting for transfers between devices: none -> 114 us  [local(): parts = lax.all_gather(cross_gram, 'pts', axis=0, tiled=False)]
    psum x1 -> x0, waiting for transfers between devices: 90.1 us -> none  [local(): summed = lax.psum(cross_gram, 'pts')]
where the time goes in v1:
time: 563 us; the launch traced here: 557 us
  other arithmetic  249 us (44%)
  matrix products  160 us (28%)
  waiting for transfers between devices  114 us (20%)
  between operations  13.8 us (2%)
  loops' own time  10.9 us (2%)
  local copies, waits for them, and re-layouts  9.6 us (2%)
    dot_general x128, matrix products, back_step(): jnp.einsum('fj,fjk->fk', factor_row, solved, precision=lax.Precision.HIGH...  119 us
    all_gather x1, waiting for transfers between devices, local(): parts = lax.all_gather(cross_gram, 'pts', axis=0, tiled=False)  114 us
    add x128, other arithmetic, eliminate(): factor = factor + scaled[:, None, :] * picker[None, :, None]  81.9 us
    reduce_sum x128, other arithmetic, eliminate(): current = jnp.sum(working * picker[None, None, :], axis=2) * below[None, :]  44.1 us
    reduce_sum x128, other arithmetic, back_step(): factor_row = jnp.sum(upper_factor * picker[None, :, None], axis=1)  33.5 us
    add x128, other arithmetic, back_step(): return solved + picker[None, :, None] * value[:, None, :]  25.8 us
    dot_general x10, matrix products, gram_of(): jnp.einsum('fki,fkj->fij', upper_factor, upper_factor, precision=lax.Prec...  19.4 us
    reduce_sum x128, other arithmetic, eliminate(): pivot = jnp.sqrt(jnp.sum(current * picker[None, :], axis=1))  14.6 us
  transfers between devices with their start and end apart: 1, of which 1 were waited for; matrix products, arithmetic and copies ran while one was open for 0% of the time, Pallas kernels for 0%

profile of v1, /device:TPU:0, one launch (start us, length us, event | category | flops | bytes accessed | tf_op | source)
XLA Modules:
  0.0 556.8 jit_solution(7274754145352786880)
XLA Ops:
  7.2 4.0 multiply_convert_fusion
  11.3 1.6 fusion.23
  13.3 1.3 maximum_maximum_fusion
  14.6 114.0 %all-gather.3.cloned.1.call-done = f32[256,128,128]{2,1,0:T(8,128)} async-done(((f32[16,128,128]{2,1,0:T(8,128)}), f32[256,128,128]{2,1,0:T(8,128)}) %all-gather.3.cloned.1.call-update) | async-done | bytes 16777232 | tf_op jit(solution)/shard_map/all_gather | solution.py:75
  128.6 7.4 %reduce_sum.83 = f32[16,128,128]{2,1,0:T(8,128)S(1)} reduce(f32[16,16,128,128]{3,2,1,0:T(8,128)} %bitcast.62, f32[]{:T(128)} %constant.44.clone.1), dimensions={0}, to_apply=%region_0.0 | reduce | flops 3932160 | bytes 17825796 | tf_op jit(solution)/shard_map/reduce_sum | solution.py:76
  136.0 157.7 %while.32 = (s32[]{:T(128)}, f32[16,128,128]{2,1,0:T(8,128)S(1)}, f32[16,128,128]{2,1,0:T(8,128)S(1)}, s32[]{:T(128)}, s32[]{:T(128)}) while((s32[]{:T(128)}, f32[16,128,128]{2,1,0:T(8,128)S(1)}, f32[16,128,128]{2,1,0:T(8,128)S(1)}, s32[]{:T(128)}, s32[]{:T(128)}) %tuple.73), condition=%wide.region_4.0_spmd.clone.clone, body=%wide.region_1.0_spmd.clone.clone.sunk | while | flops 1843699 | bytes 5287755 | solution.py:40
  294.0 1.9 fusion.21
  295.9 1.4 fusion.18
  297.3 1.9 fusion.24
  299.2 1.3 fusion.17
  300.5 1.9 fusion.25
  302.4 1.3 fusion.16
  303.7 1.9 fusion.26
  305.7 1.5 fusion.15
  307.1 1.9 fusion.27
  309.1 1.3 fusion.14
  310.4 1.9 fusion.28
  312.3 1.3 fusion.13
  313.6 1.9 fusion.29
  315.5 1.3 fusion.12
  316.9 2.1 fusion.30
  319.0 1.3 fusion.11
  320.3 1.9 fusion.31
  322.2 1.3 fusion.10
  323.5 1.9 fusion.32
  325.5 1.3 fusion.9
  326.8 208.8 %while.31 = (s32[]{:T(128)}, f32[16,128,128]{2,1,0:T(8,128)S(1)}, f32[16,128,128]{2,1,0:T(8,128)S(1)}, f32[16,128,128]{2,1,0:T(8,128)S(1)}, s32[]{:T(128)}, /*index=5*/s32[]{:T(128)}, s32[]{:T(128)}) while((s32[]{:T(128)}, f32[16,128,128]{2,1,0:T(8,128)S(1)}, f32[16,128,128]{2,1,0:T(8,128)S(1)}, f32[16,128,128]{2,1,0:T(8,128)S(1)}, ...), condition=%wide.region_10.0_spmd.clone, body=%wide.region_6.0_spmd.clone.sunk | while | flops 5247220 | bytes 5318888 | solution.py:58
  327.1 0.9 fusion.79
  328.7 0.9 fusion.79
  330.3 0.9 fusion.79
  331.9 0.9 fusion.79
  333.6 0.9 fusion.79
  335.2 0.9 fusion.79
  336.8 0.9 fusion.79
  338.5 0.9 fusion.79
  340.1 0.9 fusion.79
  341.7 0.9 fusion.79
  343.4 0.9 fusion.79
  345.0 0.9 fusion.79
  346.6 0.9 fusion.79
  349.9 0.9 fusion.79
  351.5 0.9 fusion.79
  353.1 0.9 fusion.79
  354.8 0.9 fusion.79
  356.4 0.9 fusion.79
  358.0 0.9 fusion.79
  535.5 6.4 %convert_bitcast_fusion = bf16[16,5,256,128]{2,3,1,0:T(8,128)(2,1)} fusion(bf16[16,5,256,128]{3,2,1,0:T(8,128)(2,1)} %param.6, f32[16,128,128]{2,1,0:T(8,128)S(1)} %get-tuple-element.182), kind=kOutput, calls=%fused_computation.21 | convolution fusion | flops 673972224 | bytes 11534336 | tf_op jit(solution)/shard_map/fvpc,fcd->fvpd/dot_general | solution.py:86
  541.9 7.8 %copy.21 = bf16[16,5,256,128]{3,2,1,0:T(8,128)(2,1)} copy(bf16[16,5,256,128]{2,3,1,0:T(8,128)(2,1)} %convert_bitcast_fusion) | data formatting | bytes 10485760 | tf_op jit(solution)/shard_map/convert_element_type | solution.py:87
  (1525 shorter events, 339.1 us)
Async XLA Ops:
  6.5 122.0 %all-gather.3.cloned.1.call-start = ((), (), s32[]{:S(2)}) async-start(), calls=%async_computation | async-start | bytes 17825792 | tf_op jit(solution)/shard_map/all_gather | solution.py:75
Sparse Core Ops, SparseCore 0:
  14.7 113.8 all-gather.2
